TPU v7x, 32 devices: a whole 2x2x4 slice. The times are simulated.
32 devices in a mesh: tx: 2 (over core), ty: 4 (over y, x), lz: 4 (over z).
Axes of the slice: x: 2, y: 2, z: 4, core: 2. Of those that a mesh axis runs over, the one named last changes fastest.
Arguments:
- test_field: bfloat16 [64, 6, 48, 512], P('tx', None, 'lz', 'ty'), may hold values from -6 to 6
- dir_field: bfloat16 [64, 6, 48, 512], P('tx', None, 'lz', 'ty'), may hold values from -6 to 6
- border_b: bfloat16 [64, 6, 48, 512], P('tx', None, 'lz', 'ty')
- border_c: bfloat16 [64, 6, 48, 512], P('tx', None, 'lz', 'ty')
- land_mask: int32 [64, 512], P('tx', 'ty'), may hold values from 0 to 1, as said below
- active_rows: int32 [64, 4], P('tx', 'ty'), may hold values from -1 to 31, as said below
- cell_blocks: bfloat16 [64, 36, 512], P('tx', None, 'ty'), may hold values from -2.5 to 2.5
- column_k: bfloat16 [288, 288], replicated, may hold values from -0.375 to 0.375
- kappa: float32 [6], replicated, may hold values from 0.2 to 1
Outputs:
- test_image: bfloat16 [64, 6, 48, 512], P('tx', None, 'lz', 'ty')
- dir_image: bfloat16 [64, 6, 48, 512], P('tx', None, 'lz', 'ty')
- border: float32 [3], replicated
Inputs may be any that keep to these rules, and one draw needn't show every extreme that they name: `active_rows`: in each tile the 32 entries name distinct local rows, the active ones, followed by -1 for the rest; some tile has all 32 rows active. `land_mask`: cells whose latitude index y has y % 128 equal to 0 or 127 are ocean.
All inputs are finite; a program needn't handle non-finite values.
Results may differ from a plain program's by a relative error of at most 0.0028.
Values may be sent and summed in bfloat16 or wider, within the bound.
A program may use at most 192 MiB of HBM per device.

v0:
```python
import functools
import jax
import jax.numpy as jnp
from jax import lax
from jax.experimental import pallas as pl
from jax.experimental.pallas import tpu as pltpu
from jax.sharding import PartitionSpec as P

MESH = pl.DeviceIdType.MESH
F32 = jnp.float32
BF16 = jnp.bfloat16


MARGIN = 8


def dense_kernel(
    sizes, chunks, units,
    test_hbm, dir_hbm, b_hbm, c_hbm, land_ref, active_ref, blocks_hbm, k_hbm, kappa_ref,
    out_t, out_d, border_ref,
    test_ref, dir_ref, b_ref, c_ref, blocks_ref, k_ref,
    masked, arrived, product, coupled, weight, big_k, field, back, before_image, halo,
    edge_out, edge_in, edge_f, stat_out, stat_z, stat_y,
    ls, fs, fr, bs, br, xs, xr, ys, yr, ss, sr_z, sr_y,
):
    nx, ny, nz = sizes
    slab, rows, cells = test_ref.shape
    layers = slab // units
    full = 2 * slab
    group = rows // nz
    step = group // chunks
    pitch = rows + 2 * MARGIN
    mx, my, mz = lax.axis_index("tx"), lax.axis_index("ty"), lax.axis_index("lz")
    fields = (test_ref, dir_ref)
    outs = (out_t, out_d)

    loads = [
        pltpu.make_async_copy(source, target, ls.at[i])
        for i, (source, target) in enumerate((
            (test_hbm, test_ref), (dir_hbm, dir_ref), (k_hbm, k_ref), (b_hbm, b_ref),
            (c_hbm, c_ref), (blocks_hbm, blocks_ref),
        ))
    ]
    for load in loads:
        load.start()

    barrier = pltpu.get_barrier_semaphore()
    for k in range(1, nz):
        pl.semaphore_signal(
            barrier, inc=1, device_id={"lz": lax.rem(mz + k, nz)}, device_id_type=MESH
        )
    for k in range(1, nx * ny):
        near = {"ty": lax.rem(my + k // nx, ny), "tx": lax.rem(mx + k % nx, nx)}
        pl.semaphore_signal(barrier, inc=1, device_id=near, device_id_type=MESH)

    lane = lax.broadcasted_iota(jnp.int32, (rows, cells), 1)
    line = lax.broadcasted_iota(jnp.int32, (rows, rows), 0)
    named = jnp.max(
        jnp.where(jnp.broadcast_to(active_ref[...], (rows, rows)) == line, 1.0, 0.0),
        axis=1, keepdims=True,
    )
    weight[...] = land_ref[...].astype(F32) * named
    ocean = weight[...]

    def middle(q):
        return pl.ds(pl.multiple_of(q * pitch + MARGIN, 8), rows)

    for f in range(2):
        loads[f].wait()

        def mask(j, carry):
            field[middle(f * slab + j), :] = fields[f][j].astype(F32) * ocean
            return carry

        lax.fori_loop(0, slab, mask, 0, unroll=8)

    def pack(c):
        def pack_row(i, carry):
            x = lax.div(i, step) * group + c * step + lax.rem(i, step)
            masked[x] = field[pl.ds(MARGIN + x, full, stride=pitch), :].astype(BF16)
            return carry

        lax.fori_loop(0, nz * step, pack_row, 0, unroll=4)

    pack(0)

    pl.semaphore_wait(barrier, nx * ny + nz - 2)

    def forward(c, k):
        to = lax.rem(mz + k, nz)
        return pltpu.make_async_remote_copy(
            src_ref=masked.at[pl.ds(to * group + c * step, step)],
            dst_ref=arrived.at[c, mz],
            send_sem=fs.at[c, to],
            recv_sem=fr.at[c, mz],
            device_id={"lz": to},
            device_id_type=MESH,
        )

    def forward_in(c, k):
        src = lax.rem(mz + nz - k, nz)
        return pltpu.make_async_remote_copy(
            src_ref=arrived.at[c, src],
            dst_ref=arrived.at[c, src],
            send_sem=fs.at[c, src],
            recv_sem=fr.at[c, src],
            device_id={"lz": src},
            device_id_type=MESH,
        )

    def backward(c, k):
        to = lax.rem(mz + k, nz)
        return pltpu.make_async_remote_copy(
            src_ref=product.at[c, to],
            dst_ref=coupled.at[pl.ds(mz * group + c * step, step)],
            send_sem=bs.at[c, to],
            recv_sem=br.at[c, mz],
            device_id={"lz": to},
            device_id_type=MESH,
        )

    def backward_in(c, k):
        src = lax.rem(mz + nz - k, nz)
        return pltpu.make_async_remote_copy(
            src_ref=product.at[c, src],
            dst_ref=coupled.at[pl.ds(src * group + c * step, step)],
            send_sem=bs.at[c, src],
            recv_sem=br.at[c, src],
            device_id={"lz": src},
            device_id_type=MESH,
        )

    order = sorted(range(1, nz), key=lambda k: -min(k, nz - k))
    for c in range(1, chunks):
        pack(c)
        for k in order:
            forward(c - 1, k).start()

    def own_row(i, carry):
        arrived[lax.div(i, step), mz, lax.rem(i, step)] = masked[mz * group + i]
        return carry

    lax.fori_loop(0, group, own_row, 0)
    for k in order:
        forward(chunks - 1, k).start()
    later, before = lax.rem(mx + 1, nx), lax.rem(mx + nx - 1, nx)
    to_later = pltpu.make_async_remote_copy(
        src_ref=masked.at[rows - 1], dst_ref=halo.at[0], send_sem=xs.at[0], recv_sem=xr.at[0],
        device_id={"tx": later}, device_id_type=MESH,
    )
    to_before = pltpu.make_async_remote_copy(
        src_ref=masked.at[0], dst_ref=halo.at[1], send_sem=xs.at[1], recv_sem=xr.at[1],
        device_id={"tx": before}, device_id_type=MESH,
    )
    to_later.start()
    to_before.start()
    for f in range(2):
        def edges(j, carry):
            first, last = carry
            value = field[middle(f * slab + j), :]
            first = jnp.where(lane == j, pltpu.roll(value, j, 1), first)
            last = jnp.where(lane == j, pltpu.roll(value, j + 1, 1), last)
            return first, last

        blank = jnp.zeros((rows, cells), F32)
        first, last = lax.fori_loop(0, slab, edges, (blank, blank), unroll=4)
        edge_out[0, f] = first.astype(BF16)
        edge_out[1, f] = last.astype(BF16)

    up, down = lax.rem(my + 1, ny), lax.rem(my + ny - 1, ny)
    to_up = pltpu.make_async_remote_copy(
        src_ref=edge_out.at[1], dst_ref=edge_in.at[0], send_sem=ys.at[0], recv_sem=yr.at[0],
        device_id={"ty": up}, device_id_type=MESH,
    )
    to_down = pltpu.make_async_remote_copy(
        src_ref=edge_out.at[0], dst_ref=edge_in.at[1], send_sem=ys.at[1], recv_sem=yr.at[1],
        device_id={"ty": down}, device_id_type=MESH,
    )
    col = units * layers * nz
    wide = nz * full

    def chooser(shape, dim, f):
        i = lax.broadcasted_iota(jnp.int32, shape, dim)
        j = lax.broadcasted_iota(jnp.int32, shape, 1 - dim)
        part, rest = i // full, lax.rem(i, full)
        field, entry = rest // slab, lax.rem(rest, slab)
        unit, layer = entry // layers, lax.rem(entry, layers)
        target = unit * (layers * nz) + part * layers + layer
        return jnp.where((target == j) & (field == f), 1.0, 0.0).astype(BF16)

    loads[2].wait()
    dense = k_ref[...]
    total = None
    for f in range(2):
        left = jnp.dot(
            chooser((wide, col), 0, f), dense, preferred_element_type=F32
        ).astype(BF16)
        both = jnp.dot(left, chooser((col, wide), 1, f), preferred_element_type=F32)
        total = both if total is None else total + both
    big_k[...] = total.astype(BF16)
    to_up.start()
    to_down.start()

    for load in loads[3:]:
        load.wait()
    zero = jnp.zeros((rows, cells), F32)
    sums = (zero, zero, zero)

    def norms(j, carry):
        bb, cc, cv = carry
        b = b_ref[j].astype(F32)
        c = c_ref[j].astype(F32)
        return bb + b * b, cc + c * c, cv + c * test_ref[j].astype(F32)

    quarter = slab // chunks
    for c in range(chunks):
        for k in order:
            forward_in(c, k).wait_recv()
        part = jnp.concatenate(
            [arrived[c, :, r].reshape(wide, cells) for r in range(step)], axis=1
        )
        result = jnp.dot(big_k[...], part, preferred_element_type=F32).astype(BF16)
        for d in range(nz):
            for r in range(step):
                product[c, d, r] = result[d * full:(d + 1) * full, r * cells:(r + 1) * cells]
        sums = lax.fori_loop(c * quarter, (c + 1) * quarter, norms, sums, unroll=2)
        for k in order:
            backward(c, k).start()
        for r in range(step):
            coupled[mz * group + c * step + r] = product[c, mz, r]

    to_later.wait_recv()
    to_before.wait_recv()
    to_up.wait_recv()
    to_down.wait_recv()
    field[pl.ds(MARGIN - 1, full, stride=pitch), :] = halo[0].astype(F32)
    field[pl.ds(MARGIN + rows, full, stride=pitch), :] = halo[1].astype(F32)

    @pl.when(my > 0)
    def _():
        edge_f[0] = edge_in[0].astype(F32)

    @pl.when(my == 0)
    def _():
        edge_f[0] = jnp.zeros((2, rows, cells), F32)

    @pl.when(my < ny - 1)
    def _():
        edge_f[1] = edge_in[1].astype(F32)

    @pl.when(my == ny - 1)
    def _():
        edge_f[1] = jnp.zeros((2, rows, cells), F32)

    for f in range(2):
        for u in range(units):
            def local(z, carry):
                j = u * layers + z
                q = f * slab + j
                here = field[middle(q), :]
                south = jnp.where(
                    lane == 0, pltpu.roll(edge_f[0, f], lax.rem(cells - j, cells), 1),
                    pltpu.roll(here, 1, 1),
                )
                north = jnp.where(
                    lane == cells - 1, pltpu.roll(edge_f[1, f], cells - 1 - j, 1),
                    pltpu.roll(here, cells - 1, 1),
                )
                near = field[pl.ds(q * pitch + MARGIN - 1, rows), :]
                near = near + field[pl.ds(q * pitch + MARGIN + 1, rows), :]
                value = kappa_ref[u] * (near + south + north - 4.0 * here)
                for w in range(units):
                    value = value + blocks_ref[units * u + w].astype(F32) * field[
                        middle(f * slab + w * layers + z), :
                    ]
                before_image[q] = value
                return carry

            lax.fori_loop(0, layers, local, 0, unroll=2)

    def insert(x, carry):
        back[pl.ds(x, full, stride=rows), :] = coupled[x].astype(F32)
        return carry

    for c in range(chunks):
        for k in order:
            backward_in(c, k).wait_recv()

        def chunk_row(i, carry):
            return insert(lax.div(i, step) * group + c * step + lax.rem(i, step), carry)

        lax.fori_loop(0, nz * step, chunk_row, 0, unroll=4)

    def image(j, carry):
        ba, be = carry
        b = b_ref[j].astype(F32)
        images = []
        for f in range(2):
            q = f * slab + j
            coup = back[pl.ds(pl.multiple_of(q * rows, 8), rows), :]
            images.append(ocean * (coup + before_image[q]))
            outs[f][j] = images[f].astype(BF16)
        return ba + b * images[0], be + b * images[1]

    pair = lax.fori_loop(0, slab, image, (zero, zero), unroll=6)

    lines = [jnp.sum(v, axis=0, keepdims=True) for v in (*sums, *pair)]
    value = jnp.concatenate(lines + [jnp.zeros((3, cells), F32)], axis=0)
    base = 0
    plane = [(i, k) for i in range(ny) for k in range(nx)]
    stages = (
        ([{"lz": lax.rem(mz + k, nz)} for k in range(nz)], nz, stat_z, sr_z, mz,
         [lax.rem(mz + nz - k, nz) for k in range(nz)]),
        ([{"ty": lax.rem(my + i, ny), "tx": lax.rem(mx + k, nx)} for i, k in plane],
         ny * nx, stat_y, sr_y, my * nx + mx,
         [lax.rem(my + ny - i, ny) * nx + lax.rem(mx + nx - k, nx) for i, k in plane]),
    )
    sends = []
    for s, (peers, size, box, sem, me, sources) in enumerate(stages):
        stat_out[s] = value
        box[me] = value
        for k in range(1, size):
            copy = pltpu.make_async_remote_copy(
                src_ref=stat_out.at[s], dst_ref=box.at[me], send_sem=ss.at[base + k - 1],
                recv_sem=sem.at[me], device_id=peers[k], device_id_type=MESH,
            )
            copy.start()
            sends.append(copy)
        base += size - 1
        for k in range(1, size):
            src = sources[k]
            pltpu.make_async_remote_copy(
                src_ref=stat_out.at[s], dst_ref=box.at[src], send_sem=ss.at[0],
                recv_sem=sem.at[src], device_id=peers[k], device_id_type=MESH,
            ).wait_recv()
        value = box[0]
        for i in range(1, size):
            value = value + box[i]
    final = jnp.broadcast_to(jnp.sum(value, axis=1, keepdims=True), (8, cells))
    bb, cc, cv, ba, be = (final[i:i + 1] for i in range(5))
    line = lax.broadcasted_iota(jnp.int32, (1, cells), 1)
    top = jnp.where(line == 0, ba, jnp.where(line == 1, be, cv))
    low = jnp.where(line == 2, cc, bb)
    border_ref[...] = top / jnp.sqrt(low)

    for c in range(chunks):
        for k in order:
            forward(c, k).wait_send()
            backward(c, k).wait_send()
    to_later.wait_send()
    to_before.wait_send()
    to_up.wait_send()
    to_down.wait_send()
    for copy in sends:
        copy.wait_send()


def fast_kernel(
    sizes, span, units,
    test_hbm, dir_hbm, b_hbm, c_hbm, land_ref, active_ref, blocks_hbm, k_hbm, kappa_ref,
    out_t, out_d, border_ref, flag_ref,
    test_ref, dir_ref, b_ref, c_ref, blocks_ref, k_ref,
    wide_ref, pick, packed, arrived, product, coupled, partial, weight, place, big_k, field, back,
    before_image, halo_out, halo, edge_out, edge_in, edge_f, stat_out, stat_z, stat_y,
    ls, fs, fr, bs, br, xs, xr, ys, yr, ss, sr_z, sr_y,
):
    nx, ny, nz = sizes
    slab, rows, cells = test_ref.shape
    layers = slab // units
    full = 2 * slab
    halves = rows // span
    slots = packed.shape[0] * nz // halves
    per = slots // nz
    chunks = halves * per
    pitch = rows + 2 * MARGIN
    quad = nz * cells
    mx, my, mz = lax.axis_index("tx"), lax.axis_index("ty"), lax.axis_index("lz")
    fields = (test_ref, dir_ref)
    outs = (out_t, out_d)

    loads = [
        pltpu.make_async_copy(source, target, ls.at[i])
        for i, (source, target) in enumerate((
            (test_hbm, test_ref), (dir_hbm, dir_ref), (k_hbm, k_ref), (b_hbm, b_ref),
            (c_hbm, c_ref), (blocks_hbm, blocks_ref),
        ))
    ]
    for load in loads:
        load.start()

    barrier = pltpu.get_barrier_semaphore()
    for k in range(1, nz):
        pl.semaphore_signal(
            barrier, inc=1, device_id={"lz": lax.rem(mz + k, nz)}, device_id_type=MESH
        )
    for k in range(1, nx * ny):
        near = {"ty": lax.rem(my + k // nx, ny), "tx": lax.rem(mx + k % nx, nx)}
        pl.semaphore_signal(barrier, inc=1, device_id=near, device_id_type=MESH)

    lane = lax.broadcasted_iota(jnp.int32, (rows, cells), 1)
    line = lax.broadcasted_iota(jnp.int32, (rows, rows), 0)
    named = jnp.max(
        jnp.where(jnp.broadcast_to(active_ref[...], (rows, rows)) == line, 1.0, 0.0),
        axis=1, keepdims=True,
    )
    ocean = land_ref[...].astype(F32) * named
    weight[...] = ocean

    wet = ocean.astype(BF16)
    other = lax.broadcasted_iota(jnp.int32, (rows, rows), 1)
    earlier = jnp.where((other < line) & (other // span == line // span), 1.0, 0.0).astype(BF16)
    cell_i = lax.broadcasted_iota(jnp.int32, (cells, cells), 0)
    cell_j = lax.broadcasted_iota(jnp.int32, (cells, cells), 1)
    ahead = jnp.where(cell_i < cell_j, 1.0, 0.0).astype(BF16)
    above = jnp.dot(earlier, wet, preferred_element_type=F32).astype(BF16)
    count = jnp.dot(wet, ahead, preferred_element_type=F32)
    count = count + jnp.dot(above, jnp.ones((cells, cells), BF16), preferred_element_type=F32)
    place[...] = jnp.where(ocean > 0.0, count, -1.0)
    excess = jnp.where((ocean > 0.0) & (count >= float(slots * cells)), 1.0, 0.0)

    spot = lax.broadcasted_iota(jnp.int32, (quad, cells), 0).astype(F32)

    def choose(h, s):
        def one(i, carry):
            where = place[pl.ds(h * span + i, 1), :] - float(s * quad)
            hit = jnp.where(jnp.broadcast_to(where, (quad, cells)) == spot, 1.0, 0.0)
            pick[h * per + s, :, pl.ds(pl.multiple_of(i * cells, cells), cells)] = hit.astype(BF16)
            return carry

        lax.fori_loop(nz * s, span, one, 0, unroll=2)

    choose(0, 0)

    def middle(q, start, size):
        return pl.ds(pl.multiple_of(q * pitch + MARGIN + start, 8), size)

    def prepare(h):
        part = weight[h * span:(h + 1) * span, :]
        for f in range(2):
            def mask(j, carry):
                value = fields[f][j, h * span:(h + 1) * span, :].astype(F32) * part
                field[middle(f * slab + j, h * span, span), :] = value
                return carry

            lax.fori_loop(0, slab, mask, 0, unroll=8)

        def pack_row(i, carry):
            row = field[pl.ds(MARGIN + h * span + i, full, stride=pitch), :].astype(BF16)
            wide_ref[h, :, pl.ds(pl.multiple_of(i * cells, cells), cells)] = row
            return carry

        lax.fori_loop(0, span, pack_row, 0, unroll=4)

    def compact(h, s):
        c = h * per + s
        found = lax.dot_general(
            wide_ref[h, :, s * quad:span * cells], pick[c, :, s * quad:span * cells],
            (((1,), (1,)), ((), ())), preferred_element_type=F32,
        ).astype(BF16)
        for d in range(nz):
            packed[c, d] = found[:, d * cells:(d + 1) * cells]

    def forward(c, k):
        to = lax.rem(mz + k, nz)
        return pltpu.make_async_remote_copy(
            src_ref=packed.at[c, to], dst_ref=arrived.at[c, mz], send_sem=fs.at[c, to],
            recv_sem=fr.at[c, mz], device_id={"lz": to}, device_id_type=MESH,
        )

    def forward_in(c, k):
        src = lax.rem(mz + nz - k, nz)
        return pltpu.make_async_remote_copy(
            src_ref=arrived.at[c, src], dst_ref=arrived.at[c, src], send_sem=fs.at[c, src],
            recv_sem=fr.at[c, src], device_id={"lz": src}, device_id_type=MESH,
        )

    def backward(c, k):
        to = lax.rem(mz + k, nz)
        return pltpu.make_async_remote_copy(
            src_ref=product.at[c, to], dst_ref=coupled.at[c, mz], send_sem=bs.at[c, to],
            recv_sem=br.at[c, mz], device_id={"lz": to}, device_id_type=MESH,
        )

    def backward_in(c, k):
        src = lax.rem(mz + nz - k, nz)
        return pltpu.make_async_remote_copy(
            src_ref=product.at[c, src], dst_ref=coupled.at[c, src], send_sem=bs.at[c, src],
            recv_sem=br.at[c, src], device_id={"lz": src}, device_id_type=MESH,
        )

    order = sorted(range(1, nz), key=lambda k: -min(k, nz - k))
    loads[0].wait()
    loads[1].wait()
    for h in range(halves):
        prepare(h)
        for s in range(per):
            c = h * per + s
            if c:
                choose(h, s)
            compact(h, s)
            if c == 0:
                pl.semaphore_wait(barrier, nx * ny + nz - 2)
            for k in order:
                forward(c, k).start()
            arrived[c, mz] = packed[c, mz]

    halo_out[0] = wide_ref[halves - 1, :, (span - 1) * cells:span * cells]
    halo_out[1] = wide_ref[0, :, :cells]
    later, before = lax.rem(mx + 1, nx), lax.rem(mx + nx - 1, nx)
    to_later = pltpu.make_async_remote_copy(
        src_ref=halo_out.at[0], dst_ref=halo.at[0], send_sem=xs.at[0], recv_sem=xr.at[0],
        device_id={"tx": later}, device_id_type=MESH,
    )
    to_before = pltpu.make_async_remote_copy(
        src_ref=halo_out.at[1], dst_ref=halo.at[1], send_sem=xs.at[1], recv_sem=xr.at[1],
        device_id={"tx": before}, device_id_type=MESH,
    )
    to_later.start()
    to_before.start()
    for f in range(2):
        def edges(j, carry):
            first, last = carry
            value = field[middle(f * slab + j, 0, rows), :]
            first = jnp.where(lane == j, pltpu.roll(value, j, 1), first)
            last = jnp.where(lane == j, pltpu.roll(value, j + 1, 1), last)
            return first, last

        blank = jnp.zeros((rows, cells), F32)
        first, last = lax.fori_loop(0, slab, edges, (blank, blank), unroll=4)
        edge_out[0, f] = first.astype(BF16)
        edge_out[1, f] = last.astype(BF16)

    up, down = lax.rem(my + 1, ny), lax.rem(my + ny - 1, ny)
    to_up = pltpu.make_async_remote_copy(
        src_ref=edge_out.at[1], dst_ref=edge_in.at[0], send_sem=ys.at[0], recv_sem=yr.at[0],
        device_id={"ty": up}, device_id_type=MESH,
    )
    to_down = pltpu.make_async_remote_copy(
        src_ref=edge_out.at[0], dst_ref=edge_in.at[1], send_sem=ys.at[1], recv_sem=yr.at[1],
        device_id={"ty": down}, device_id_type=MESH,
    )
    col = units * layers * nz
    wide = nz * full

    def chooser(shape, dim, f):
        i = lax.broadcasted_iota(jnp.int32, shape, dim)
        j = lax.broadcasted_iota(jnp.int32, shape, 1 - dim)
        part, rest = i // full, lax.rem(i, full)
        field, entry = rest // slab, lax.rem(rest, slab)
        unit, layer = entry // layers, lax.rem(entry, layers)
        target = unit * (layers * nz) + part * layers + layer
        return jnp.where((target == j) & (field == f), 1.0, 0.0).astype(BF16)

    loads[2].wait()
    dense = k_ref[...]
    total = None
    for f in range(2):
        left = jnp.dot(
            chooser((wide, col), 0, f), dense, preferred_element_type=F32
        ).astype(BF16)
        both = jnp.dot(left, chooser((col, wide), 1, f), preferred_element_type=F32)
        total = both if total is None else total + both
    big_k[...] = total.astype(BF16)
    to_up.start()
    to_down.start()

    for load in loads[3:]:
        load.wait()
    zero = jnp.zeros((rows, cells), F32)
    sums = (zero, zero, zero)

    def norms(j, carry):
        bb, cc, cv = carry
        b = b_ref[j].astype(F32)
        c = c_ref[j].astype(F32)
        return bb + b * b, cc + c * c, cv + c * test_ref[j].astype(F32)

    share = slab // chunks
    for c in range(chunks):
        for k in order:
            forward_in(c, k).wait_recv()
        part = arrived[c].reshape(wide, cells)
        result = jnp.dot(big_k[...], part, preferred_element_type=F32).astype(BF16)
        for d in range(nz):
            product[c, d] = result[d * full:(d + 1) * full]
        for k in order:
            backward(c, k).start()
        coupled[c, mz] = product[c, mz]
        sums = lax.fori_loop(c * share, (c + 1) * share, norms, sums, unroll=2)
    if share * chunks < slab:
        sums = lax.fori_loop(share * chunks, slab, norms, sums)

    to_later.wait_recv()
    to_before.wait_recv()
    to_up.wait_recv()
    to_down.wait_recv()
    field[pl.ds(MARGIN - 1, full, stride=pitch), :] = halo[0].astype(F32)
    field[pl.ds(MARGIN + rows, full, stride=pitch), :] = halo[1].astype(F32)

    @pl.when(my > 0)
    def _():
        edge_f[0] = edge_in[0].astype(F32)

    @pl.when(my == 0)
    def _():
        edge_f[0] = jnp.zeros((2, rows, cells), F32)

    @pl.when(my < ny - 1)
    def _():
        edge_f[1] = edge_in[1].astype(F32)

    @pl.when(my == ny - 1)
    def _():
        edge_f[1] = jnp.zeros((2, rows, cells), F32)

    for f in range(2):
        for u in range(units):
            def local(z, carry):
                j = u * layers + z
                q = f * slab + j
                here = field[middle(q, 0, rows), :]
                south = jnp.where(
                    lane == 0, pltpu.roll(edge_f[0, f], lax.rem(cells - j, cells), 1),
                    pltpu.roll(here, 1, 1),
                )
                north = jnp.where(
                    lane == cells - 1, pltpu.roll(edge_f[1, f], cells - 1 - j, 1),
                    pltpu.roll(here, cells - 1, 1),
                )
                near = field[pl.ds(q * pitch + MARGIN - 1, rows), :]
                near = near + field[pl.ds(q * pitch + MARGIN + 1, rows), :]
                value = kappa_ref[u] * (near + south + north - 4.0 * here)
                for w in range(units):
                    value = value + blocks_ref[units * u + w].astype(F32) * field[
                        middle(f * slab + w * layers + z, 0, rows), :
                    ]
                before_image[q] = value
                return carry

            lax.fori_loop(0, layers, local, 0, unroll=2)

    none = jnp.zeros((span, cells), F32)
    pair = (none, none)
    for h in range(halves):
        for s in range(per):
            c = h * per + s
            for k in order:
                backward_in(c, k).wait_recv()
            block = jnp.concatenate([coupled[c, d] for d in range(nz)], axis=1)
            spread = jnp.dot(
                block, pick[c, :, s * quad:span * cells], preferred_element_type=F32
            )
            if s:
                spread = spread + partial[:, s * quad:span * cells]
            done = nz if s + 1 < per else span - nz * s
            for i in range(done):
                x = h * span + nz * s + i
                back[pl.ds(x, full, stride=rows), :] = spread[:, i * cells:(i + 1) * cells]
            if s + 1 < per:
                partial[:, (s + 1) * quad:span * cells] = spread[:, quad:]
        part = weight[h * span:(h + 1) * span, :]

        def image(j, carry):
            ba, be = carry
            b = b_ref[j, h * span:(h + 1) * span, :].astype(F32)
            images = []
            for f in range(2):
                q = f * slab + j
                coup = back[pl.ds(pl.multiple_of(q * rows + h * span, 8), span), :]
                images.append(part * (coup + before_image[q, h * span:(h + 1) * span, :]))
                outs[f][j, h * span:(h + 1) * span, :] = images[f].astype(BF16)
            return ba + b * images[0], be + b * images[1]

        pair = lax.fori_loop(0, slab, image, pair, unroll=6)

    lines = [jnp.sum(v, axis=0, keepdims=True) for v in (*sums, *pair, excess)]
    value = jnp.concatenate(lines + [jnp.zeros((2, cells), F32)], axis=0)
    base = 0
    plane = [(i, k) for i in range(ny) for k in range(nx)]
    stages = (
        ([{"lz": lax.rem(mz + k, nz)} for k in range(nz)], nz, stat_z, sr_z, mz,
         [lax.rem(mz + nz - k, nz) for k in range(nz)]),
        ([{"ty": lax.rem(my + i, ny), "tx": lax.rem(mx + k, nx)} for i, k in plane],
         ny * nx, stat_y, sr_y, my * nx + mx,
         [lax.rem(my + ny - i, ny) * nx + lax.rem(mx + nx - k, nx) for i, k in plane]),
    )
    sends = []
    for s, (peers, size, box, sem, me, sources) in enumerate(stages):
        stat_out[s] = value
        box[me] = value
        for k in range(1, size):
            copy = pltpu.make_async_remote_copy(
                src_ref=stat_out.at[s], dst_ref=box.at[me], send_sem=ss.at[base + k - 1],
                recv_sem=sem.at[me], device_id=peers[k], device_id_type=MESH,
            )
            copy.start()
            sends.append(copy)
        base += size - 1
        for k in range(1, size):
            src = sources[k]
            pltpu.make_async_remote_copy(
                src_ref=stat_out.at[s], dst_ref=box.at[src], send_sem=ss.at[0],
                recv_sem=sem.at[src], device_id=peers[k], device_id_type=MESH,
            ).wait_recv()
        value = box[0]
        for i in range(1, size):
            value = value + box[i]
    final = jnp.broadcast_to(jnp.sum(value, axis=1, keepdims=True), (8, cells))
    bb, cc, cv, ba, be, over = (final[i:i + 1] for i in range(6))
    line = lax.broadcasted_iota(jnp.int32, (1, cells), 1)
    top = jnp.where(line == 0, ba, jnp.where(line == 1, be, cv))
    low = jnp.where(line == 2, cc, bb)
    border_ref[...] = top / jnp.sqrt(low)
    flag_ref[0] = jnp.where(jnp.max(over) > 0.0, 1, 0)

    for c in range(chunks):
        for k in order:
            forward(c, k).wait_send()
            backward(c, k).wait_send()
    to_later.wait_send()
    to_before.wait_send()
    to_up.wait_send()
    to_down.wait_send()
    for copy in sends:
        copy.wait_send()


def dense_call(sizes, units, layers, args):
    nx, ny, nz = sizes
    slab, rows, cells = args[0].shape
    full = 2 * slab
    group = rows // nz
    chunks = 4 if group % 4 == 0 else 1
    step = group // chunks
    vmem = pl.BlockSpec(memory_space=pltpu.VMEM)
    smem = pl.BlockSpec(memory_space=pltpu.SMEM)
    hbm = pl.BlockSpec(memory_space=pl.ANY)
    dma = pltpu.SemaphoreType.DMA
    return pl.pallas_call(
        functools.partial(dense_kernel, sizes, chunks, units),
        out_shape=(
            jax.ShapeDtypeStruct((slab, rows, cells), BF16),
            jax.ShapeDtypeStruct((slab, rows, cells), BF16),
            jax.ShapeDtypeStruct((1, cells), F32),
        ),
        in_specs=[hbm] * 4 + [vmem] * 2 + [hbm] * 2 + [smem],
        out_specs=(vmem, vmem, vmem),
        scratch_shapes=[
            *[pltpu.VMEM((slab, rows, cells), BF16)] * 4,
            pltpu.VMEM(args[6].shape, BF16),
            pltpu.VMEM(args[7].shape, BF16),
            pltpu.VMEM((rows, full, cells), BF16),
            pltpu.VMEM((chunks, nz, step, full, cells), BF16),
            pltpu.VMEM((chunks, nz, step, full, cells), BF16),
            pltpu.VMEM((rows, full, cells), BF16),
            pltpu.VMEM((rows, cells), F32),
            pltpu.VMEM((nz * full, nz * full), BF16),
            pltpu.VMEM((full * (rows + 2 * MARGIN), cells), F32),
            pltpu.VMEM((full * rows, cells), F32),
            pltpu.VMEM((full, rows, cells), F32),
            pltpu.VMEM((2, full, cells), BF16),
            pltpu.VMEM((2, 2, rows, cells), BF16),
            pltpu.VMEM((2, 2, rows, cells), BF16),
            pltpu.VMEM((2, 2, rows, cells), F32),
            pltpu.VMEM((2, 8, cells), F32),
            pltpu.VMEM((nz, 8, cells), F32),
            pltpu.VMEM((ny * nx, 8, cells), F32),
            dma((6,)),
            *[dma((chunks, nz))] * 4,
            *[dma((2,))] * 4,
            dma((nx * ny + nz - 2,)),
            dma((nz,)),
            dma((ny * nx,)),
        ],
        compiler_params=pltpu.CompilerParams(
            collective_id=0, has_side_effects=True, vmem_limit_bytes=52 * 1024 * 1024
        ),
    )(*args)


def fast_call(sizes, span, units, layers, args):
    nx, ny, nz = sizes
    slab, rows, cells = args[0].shape
    full = 2 * slab
    chunks = (rows * 3 // 4) // nz
    quad = nz * cells
    vmem = pl.BlockSpec(memory_space=pltpu.VMEM)
    smem = pl.BlockSpec(memory_space=pltpu.SMEM)
    hbm = pl.BlockSpec(memory_space=pl.ANY)
    dma = pltpu.SemaphoreType.DMA
    return pl.pallas_call(
        functools.partial(fast_kernel, sizes, span, units),
        out_shape=(
            jax.ShapeDtypeStruct((slab, rows, cells), BF16),
            jax.ShapeDtypeStruct((slab, rows, cells), BF16),
            jax.ShapeDtypeStruct((1, cells), F32),
            jax.ShapeDtypeStruct((1,), jnp.int32),
        ),
        in_specs=[hbm] * 4 + [vmem] * 2 + [hbm] * 2 + [smem],
        out_specs=(vmem, vmem, vmem, smem),
        scratch_shapes=[
            *[pltpu.VMEM((slab, rows, cells), BF16)] * 4,
            pltpu.VMEM(args[6].shape, BF16),
            pltpu.VMEM(args[7].shape, BF16),
            pltpu.VMEM((rows // span, full, span * cells), BF16),
            pltpu.VMEM((chunks, quad, span * cells), BF16),
            *[pltpu.VMEM((chunks, nz, full, cells), BF16)] * 4,
            pltpu.VMEM((full, span * cells), F32),
            pltpu.VMEM((rows, cells), F32),
            pltpu.VMEM((rows, cells), F32),
            pltpu.VMEM((nz * full, nz * full), BF16),
            pltpu.VMEM((full * (rows + 2 * MARGIN), cells), F32),
            pltpu.VMEM((full * rows, cells), F32),
            pltpu.VMEM((full, rows, cells), F32),
            pltpu.VMEM((2, full, cells), BF16),
            pltpu.VMEM((2, full, cells), BF16),
            pltpu.VMEM((2, 2, rows, cells), BF16),
            pltpu.VMEM((2, 2, rows, cells), BF16),
            pltpu.VMEM((2, 2, rows, cells), F32),
            pltpu.VMEM((2, 8, cells), F32),
            pltpu.VMEM((nz, 8, cells), F32),
            pltpu.VMEM((ny * nx, 8, cells), F32),
            dma((6,)),
            *[dma((chunks, nz))] * 4,
            *[dma((2,))] * 4,
            dma((nx * ny + nz - 2,)),
            dma((nz,)),
            dma((ny * nx,)),
        ],
        compiler_params=pltpu.CompilerParams(
            collective_id=1, has_side_effects=True, vmem_limit_bytes=52 * 1024 * 1024
        ),
    )(*args)


def body(sizes, *arrays):
    nx, ny, nz = sizes
    rows, units, layers, cells = arrays[0].shape
    slab = units * layers
    wide = [v.transpose(1, 2, 0, 3).reshape(slab, rows, cells) for v in arrays[:4]]
    args = (*wide, arrays[4], arrays[5].T, arrays[6].transpose(1, 0, 2), *arrays[7:])
    args = (*[pltpu.with_memory_space_constraint(v, pltpu.HBM) for v in args[:8]], args[8])
    span = rows // 2
    if rows % 16 == 0 and (span * 3 // 4) % nz == 0:
        *quick, flag = fast_call(sizes, span, units, layers, args)
        out_t, out_d, border = lax.cond(
            flag[0] > 0, lambda: dense_call(sizes, units, layers, args), lambda: tuple(quick)
        )
    else:
        out_t, out_d, border = dense_call(sizes, units, layers, args)
    outs = [
        v.reshape(units, layers, rows, cells).transpose(2, 0, 1, 3) for v in (out_t, out_d)
    ]
    return (*outs, border[0, :3])


def solution(mesh):
    wide = P("tx", None, "lz", "ty")
    in_specs = (
        wide, wide, wide, wide, P("tx", "ty"), P("tx", "ty"), P("tx", None, "ty"), P(), P(),
    )
    sizes = tuple(mesh.shape[name] for name in ("tx", "ty", "lz"))
    return jax.shard_map(
        functools.partial(body, sizes), mesh=mesh, in_specs=in_specs,
        out_specs=(wide, wide, P()), check_vma=False,
    )
```

profile of v0, /device:TPU:0, one launch (start us, length us, event | category | flops | bytes accessed | tf_op | source)
XLA Modules:
  0.0 61.6 jit_solution(1528305428260108133)
XLA Ops:
  0.6 0.0 copy-start
  0.6 0.6 %copy-done = f32[6]{0:T(128)S(1)} copy-done((f32[6]{0:T(128)S(1)}, f32[6]{0:T(128)}, u32[]{:S(2)}) %copy-start) | copy-done | bytes 48
  1.3 57.3 %shard_map.112 = (bf16[72,32,128]{2,1,0:T(8,128)(2,1)S(1)}, bf16[72,32,128]{2,1,0:T(8,128)(2,1)S(1)}, f32[1,128]{1,0:T(1,128)S(1)}, s32[1]{0:T(128)}) custom-call(bf16[72,32,128]{2,1,0:T(8,128)(2,1)} %bitcast.23, bf16[72,32,128]{2,1,0:T(8,128)(2,1)} %bitcast.25, bf16[72,32,128]{2,1,0:T(8,128)(2,1)} %bitcast.27, bf16[72,32,128]{2,1,0:T(8,128)(2,1)} %bitcast.29, ...), custom_call_target="tpu_custom_call" | custom-call | tf_op jit(solution)/shard_map/pallas_call | solution.py:791
  59.2 0.2 conditional.1
  59.5 0.5 slice_bitcast_fusion
  60.0 0.8 %copy.20 = bf16[32,6,12,128]{3,0,2,1:T(8,128)(2,1)} copy(bf16[32,6,12,128]{3,0,2,1:T(8,128)(2,1)S(1)} %bitcast.33) | data formatting | bytes 1179648
  60.8 0.8 %copy.21 = bf16[32,6,12,128]{3,0,2,1:T(8,128)(2,1)} copy(bf16[32,6,12,128]{3,0,2,1:T(8,128)(2,1)S(1)} %bitcast.34) | data formatting | bytes 1179648
Async XLA Ops:
  0.6 0.7 %copy-start = (f32[6]{0:T(128)S(1)}, f32[6]{0:T(128)}, u32[]{:S(2)}) copy-start(f32[6]{0:T(128)} %kappa_ref.1) | copy-start | bytes 76
where the time goes:
time: 61.9 us; the launch traced here: 61.6 us
  Pallas kernels  57.3 us (93%)
  local copies, waits for them, and re-layouts  2.79 us (5%)
  between operations  1.27 us (2%)
    pallas_call x1, Pallas kernels, fast_call(): pl.pallas_call(functools.partial(fast_kernel, sizes, span, units), out_sh...  57.3 us
    unnamed x4, local copies, waits for them, and re-layouts  2.28 us

commit v1 on v0

--- a/solution.py
+++ b/solution.py
@@ -1,4 +1,6 @@
 import functools
+import itertools
+import math
 import jax
 import jax.numpy as jnp
 from jax import lax
@@ -355,16 +357,55 @@
         copy.wait_send()
 
 
+def stage_sizes(sizes):
+    names = ("lz", "ty", "tx")
+    dims = [(name, i, sizes[("tx", "ty", "lz").index(name)]) for i, name in enumerate(names)]
+    if sizes[0] * sizes[1] * sizes[2] <= 64:
+        return [dims]
+    return [dims[:1], dims[1:]]
+
+
+def put_kernel(t_ref, d_ref, border_ref, out_t, out_d, out_border, line, sems):
+    line[...] = border_ref[0, :line.shape[0]]
+    copies = [
+        pltpu.make_async_copy(source, target, sems.at[i])
+        for i, (source, target) in enumerate(((t_ref, out_t), (d_ref, out_d), (line, out_border)))
+    ]
+    for copy in copies:
+        copy.start()
+    for copy in copies:
+        copy.wait()
+
+
+def put_call(out_t, out_d, border):
+    hbm = pl.BlockSpec(memory_space=pl.ANY)
+    return pl.pallas_call(
+        put_kernel,
+        out_shape=(
+            jax.ShapeDtypeStruct(out_t.shape, BF16),
+            jax.ShapeDtypeStruct(out_d.shape, BF16),
+            jax.ShapeDtypeStruct((3,), F32),
+        ),
+        in_specs=[hbm, hbm, pl.BlockSpec(memory_space=pltpu.VMEM)],
+        out_specs=(hbm, hbm, hbm),
+        scratch_shapes=[pltpu.VMEM((3,), F32), pltpu.SemaphoreType.DMA((3,))],
+    )(out_t, out_d, border)
+
+
 def fast_kernel(
     sizes, span, units,
-    test_hbm, dir_hbm, b_hbm, c_hbm, land_ref, active_ref, blocks_hbm, k_hbm, kappa_ref,
+    test_hbm, dir_hbm, b_hbm, c_hbm, land_ref, active_ref, blocks_hbm, k_hbm, kappa_hbm,
     out_t, out_d, border_ref, flag_ref,
     test_ref, dir_ref, b_ref, c_ref, blocks_ref, k_ref,
-    wide_ref, pick, packed, arrived, product, coupled, partial, weight, place, big_k, field, back,
-    before_image, halo_out, halo, edge_out, edge_in, edge_f, stat_out, stat_z, stat_y,
-    ls, fs, fr, bs, br, xs, xr, ys, yr, ss, sr_z, sr_y,
+    kappa_ref, wide_ref, pick, packed, arrived, product, coupled, partial, weight, place, big_k,
+    field, b_field, back, before_image, halo_out, halo, edge_out, edge_in, edge_f, stat_out,
+    *rest,
 ):
     nx, ny, nz = sizes
+    stages = len(stage_sizes(sizes))
+    boxes, rest = rest[:stages], rest[stages:]
+    ls, fs, fr, bs, br, xs, xr, ys, yr, ss = rest[:10]
+    stat_sems = rest[10:]
     slab, rows, cells = test_ref.shape
     layers = slab // units
     full = 2 * slab
@@ -381,8 +422,8 @@
     loads = [
         pltpu.make_async_copy(source, target, ls.at[i])
         for i, (source, target) in enumerate((
-            (test_hbm, test_ref), (dir_hbm, dir_ref), (k_hbm, k_ref), (b_hbm, b_ref),
-            (c_hbm, c_ref), (blocks_hbm, blocks_ref),
+            (test_hbm, test_ref), (dir_hbm, dir_ref), (b_hbm, b_ref), (k_hbm, k_ref),
+            (c_hbm, c_ref), (blocks_hbm, blocks_ref), (kappa_hbm, kappa_ref),
         ))
     ]
     for load in loads:
@@ -444,9 +485,19 @@
 
             lax.fori_loop(0, slab, mask, 0, unroll=8)
 
+        def widen(j, carry):
+            start = pl.multiple_of(j * rows + h * span, 8)
+            b_field[pl.ds(start, span), :] = b_ref[j, h * span:(h + 1) * span, :].astype(F32)
+            return carry
+
+        lax.fori_loop(0, slab, widen, 0, unroll=8)
+
         def pack_row(i, carry):
+            spot = pl.ds(pl.multiple_of(i * cells, cells), cells)
             row = field[pl.ds(MARGIN + h * span + i, full, stride=pitch), :].astype(BF16)
-            wide_ref[h, :, pl.ds(pl.multiple_of(i * cells, cells), cells)] = row
+            wide_ref[h, :full, spot] = row
+            row = b_field[pl.ds(h * span + i, slab, stride=rows), :].astype(BF16)
+            wide_ref[h, full:, spot] = row
             return carry
 
         lax.fori_loop(0, span, pack_row, 0, unroll=4)
@@ -460,18 +511,25 @@
         for d in range(nz):
             packed[c, d] = found[:, d * cells:(d + 1) * cells]
 
+    def sent(c):
+        return full if c < chunks - 1 else full + slab
+
     def forward(c, k):
         to = lax.rem(mz + k, nz)
+        part = pl.ds(0, sent(c))
         return pltpu.make_async_remote_copy(
-            src_ref=packed.at[c, to], dst_ref=arrived.at[c, mz], send_sem=fs.at[c, to],
-            recv_sem=fr.at[c, mz], device_id={"lz": to}, device_id_type=MESH,
+            src_ref=packed.at[c, to, part], dst_ref=arrived.at[c, mz, part],
+            send_sem=fs.at[c, to], recv_sem=fr.at[c, mz], device_id={"lz": to},
+            device_id_type=MESH,
         )
 
     def forward_in(c, k):
         src = lax.rem(mz + nz - k, nz)
+        part = pl.ds(0, sent(c))
         return pltpu.make_async_remote_copy(
-            src_ref=arrived.at[c, src], dst_ref=arrived.at[c, src], send_sem=fs.at[c, src],
-            recv_sem=fr.at[c, src], device_id={"lz": src}, device_id_type=MESH,
+            src_ref=arrived.at[c, src, part], dst_ref=arrived.at[c, src, part],
+            send_sem=fs.at[c, src], recv_sem=fr.at[c, src], device_id={"lz": src},
+            device_id_type=MESH,
         )
 
     def backward(c, k):
@@ -489,8 +547,8 @@
         )
 
     order = sorted(range(1, nz), key=lambda k: -min(k, nz - k))
-    loads[0].wait()
-    loads[1].wait()
+    for load in loads[:3]:
+        load.wait()
     for h in range(halves):
         prepare(h)
         for s in range(per):
@@ -504,8 +562,8 @@
                 forward(c, k).start()
             arrived[c, mz] = packed[c, mz]
 
-    halo_out[0] = wide_ref[halves - 1, :, (span - 1) * cells:span * cells]
-    halo_out[1] = wide_ref[0, :, :cells]
+    halo_out[0] = wide_ref[halves - 1, :full, (span - 1) * cells:span * cells]
+    halo_out[1] = wide_ref[0, :full, :cells]
     later, before = lax.rem(mx + 1, nx), lax.rem(mx + nx - 1, nx)
     to_later = pltpu.make_async_remote_copy(
         src_ref=halo_out.at[0], dst_ref=halo.at[0], send_sem=xs.at[0], recv_sem=xr.at[0],
@@ -539,6 +597,8 @@
         src_ref=edge_out.at[0], dst_ref=edge_in.at[1], send_sem=ys.at[1], recv_sem=yr.at[1],
         device_id={"ty": down}, device_id_type=MESH,
     )
+    to_up.start()
+    to_down.start()
     col = units * layers * nz
     wide = nz * full
 
@@ -551,7 +611,7 @@
         target = unit * (layers * nz) + part * layers + layer
         return jnp.where((target == j) & (field == f), 1.0, 0.0).astype(BF16)
 
-    loads[2].wait()
+    loads[3].wait()
     dense = k_ref[...]
     total = None
     for f in range(2):
@@ -561,10 +621,8 @@
         both = jnp.dot(left, chooser((col, wide), 1, f), preferred_element_type=F32)
         total = both if total is None else total + both
     big_k[...] = total.astype(BF16)
-    to_up.start()
-    to_down.start()
-
-    for load in loads[3:]:
+
+    for load in loads[4:]:
         load.wait()
     zero = jnp.zeros((rows, cells), F32)
     sums = (zero, zero, zero)
@@ -575,77 +633,168 @@
         c = c_ref[j].astype(F32)
         return bb + b * b, cc + c * c, cv + c * test_ref[j].astype(F32)
 
+    to_later.wait_recv()
+    to_before.wait_recv()
+    to_up.wait_recv()
+    to_down.wait_recv()
+    field[pl.ds(MARGIN - 1, full, stride=pitch), :] = halo[0].astype(F32)
+    field[pl.ds(MARGIN + rows, full, stride=pitch), :] = halo[1].astype(F32)
+
+    @pl.when(my > 0)
+    def _():
+        edge_f[0] = edge_in[0].astype(F32)
+
+    @pl.when(my == 0)
+    def _():
+        edge_f[0] = jnp.zeros((2, rows, cells), F32)
+
+    @pl.when(my < ny - 1)
+    def _():
+        edge_f[1] = edge_in[1].astype(F32)
+
+    @pl.when(my == ny - 1)
+    def _():
+        edge_f[1] = jnp.zeros((2, rows, cells), F32)
+
+
+    totals = [zero, zero]
+
+    def local_part(f, u):
+        def local(z, total):
+            j = u * layers + z
+            q = f * slab + j
+            here = field[middle(q, 0, rows), :]
+            south = jnp.where(
+                lane == 0, pltpu.roll(edge_f[0, f], lax.rem(cells - j, cells), 1),
+                pltpu.roll(here, 1, 1),
+            )
+            north = jnp.where(
+                lane == cells - 1, pltpu.roll(edge_f[1, f], cells - 1 - j, 1),
+                pltpu.roll(here, cells - 1, 1),
+            )
+            near = field[pl.ds(q * pitch + MARGIN - 1, rows), :]
+            near = near + field[pl.ds(q * pitch + MARGIN + 1, rows), :]
+            value = kappa_ref[u] * (near + south + north - 4.0 * here)
+            for w in range(units):
+                value = value + blocks_ref[units * u + w].astype(F32) * field[
+                    middle(f * slab + w * layers + z, 0, rows), :
+                ]
+            before_image[q] = value
+            return total + b_ref[j].astype(F32) * value
+
+        totals[f] = lax.fori_loop(0, layers, local, totals[f], unroll=2)
+
+    jobs = [(f, u) for f in range(2) for u in range(units)]
+    each = -(-len(jobs) // chunks)
+
+    tile = jnp.zeros((8, cells), F32)
+
+    def dots(pair, values, weights):
+        ba, be = pair
+        for d in range(nz):
+            y = values[d].astype(F32)
+            b = weights[d, full:].astype(F32)
+            ba = ba + jnp.sum((y[:slab] * b).reshape(slab // 8, 8, cells), axis=0)
+            be = be + jnp.sum((y[slab:] * b).reshape(slab // 8, 8, cells), axis=0)
+        return ba, be
+
+    pair = (tile, tile)
     share = slab // chunks
     for c in range(chunks):
         for k in order:
             forward_in(c, k).wait_recv()
-        part = arrived[c].reshape(wide, cells)
+        part = jnp.concatenate([arrived[c, d, :full] for d in range(nz)], axis=0)
         result = jnp.dot(big_k[...], part, preferred_element_type=F32).astype(BF16)
         for d in range(nz):
             product[c, d] = result[d * full:(d + 1) * full]
         for k in order:
             backward(c, k).start()
         coupled[c, mz] = product[c, mz]
+        if sent(c) > full:
+            pair = dots(pair, product.at[c], arrived.at[c])
         sums = lax.fori_loop(c * share, (c + 1) * share, norms, sums, unroll=2)
+        for job in jobs[c * each:(c + 1) * each]:
+            local_part(*job)
     if share * chunks < slab:
         sums = lax.fori_loop(share * chunks, slab, norms, sums)
 
-    to_later.wait_recv()
-    to_before.wait_recv()
-    to_up.wait_recv()
-    to_down.wait_recv()
-    field[pl.ds(MARGIN - 1, full, stride=pitch), :] = halo[0].astype(F32)
-    field[pl.ds(MARGIN + rows, full, stride=pitch), :] = halo[1].astype(F32)
-
-    @pl.when(my > 0)
-    def _():
-        edge_f[0] = edge_in[0].astype(F32)
-
-    @pl.when(my == 0)
-    def _():
-        edge_f[0] = jnp.zeros((2, rows, cells), F32)
-
-    @pl.when(my < ny - 1)
-    def _():
-        edge_f[1] = edge_in[1].astype(F32)
-
-    @pl.when(my == ny - 1)
-    def _():
-        edge_f[1] = jnp.zeros((2, rows, cells), F32)
-
-    for f in range(2):
-        for u in range(units):
-            def local(z, carry):
-                j = u * layers + z
+    def image(start, stop):
+        part = weight[start:stop, :]
+
+        def one(j, carry):
+            for f in range(2):
                 q = f * slab + j
-                here = field[middle(q, 0, rows), :]
-                south = jnp.where(
-                    lane == 0, pltpu.roll(edge_f[0, f], lax.rem(cells - j, cells), 1),
-                    pltpu.roll(here, 1, 1),
-                )
-                north = jnp.where(
-                    lane == cells - 1, pltpu.roll(edge_f[1, f], cells - 1 - j, 1),
-                    pltpu.roll(here, cells - 1, 1),
-                )
-                near = field[pl.ds(q * pitch + MARGIN - 1, rows), :]
-                near = near + field[pl.ds(q * pitch + MARGIN + 1, rows), :]
-                value = kappa_ref[u] * (near + south + north - 4.0 * here)
-                for w in range(units):
-                    value = value + blocks_ref[units * u + w].astype(F32) * field[
-                        middle(f * slab + w * layers + z, 0, rows), :
-                    ]
-                before_image[q] = value
-                return carry
-
-            lax.fori_loop(0, layers, local, 0, unroll=2)
-
-    none = jnp.zeros((span, cells), F32)
-    pair = (none, none)
+                coup = back[pl.ds(pl.multiple_of(q * rows + start, 8), stop - start), :]
+                value = part * (coup + before_image[q, start:stop, :])
+                outs[f][j, start:stop, :] = value.astype(BF16)
+            return carry
+
+        lax.fori_loop(0, slab, one, 0, unroll=6)
+
+    def begin(s, value):
+        stat_out[s] = value
+        _, peers, me = reduce_stages[s]
+        boxes[s][me] = value
+        copies = []
+        for n, (peer, source) in enumerate(peers):
+            copy = pltpu.make_async_remote_copy(
+                src_ref=stat_out.at[s], dst_ref=boxes[s].at[me], send_sem=ss.at[bases[s] + n],
+                recv_sem=stat_sems[s].at[me], device_id=peer, device_id_type=MESH,
+            )
+            copy.start()
+            copies.append(copy)
+        return copies
+
+    def finish(s):
+        for n, (peer, source) in enumerate(reduce_stages[s][1]):
+            pltpu.make_async_remote_copy(
+                src_ref=stat_out.at[s], dst_ref=boxes[s].at[source],
+                send_sem=ss.at[bases[s] + n], recv_sem=stat_sems[s].at[source], device_id=peer,
+                device_id_type=MESH,
+            ).wait_recv()
+        return jnp.sum(boxes[s][...], axis=0)
+
+    reduce_stages = []
+    for dims in stage_sizes(sizes):
+        me = 0
+        for name, at, n in dims:
+            me = me * n + lax.axis_index(name)
+        peers = []
+        for shift in itertools.product(*[range(n) for _, _, n in dims]):
+            if any(shift):
+                peer = {
+                    name: lax.rem(lax.axis_index(name) + k, n)
+                    for (name, _, n), k in zip(dims, shift)
+                }
+                source = 0
+                for (name, _, n), k in zip(dims, shift):
+                    source = source * n + lax.rem(lax.axis_index(name) + n - k, n)
+                peers.append((peer, source))
+        reduce_stages.append((dims, peers, me))
+    bases = [sum(len(r[1]) for r in reduce_stages[:s]) for s in range(stages)]
+    sends = []
+
+    seat = lax.broadcasted_iota(jnp.int32, (8, cells), 0)
+    spot = lax.broadcasted_iota(jnp.int32, (8, cells), 1)
     for h in range(halves):
+        drawn = 0
         for s in range(per):
             c = h * per + s
             for k in order:
                 backward_in(c, k).wait_recv()
+            if sent(c) == full:
+                pair = dots(pair, coupled.at[c], packed.at[c])
+            if c == chunks - 2:
+                ba, be = (
+                    jnp.sum(v, axis=0, keepdims=True) + jnp.sum(w, axis=0, keepdims=True)
+                    for v, w in zip(pair, [ocean * v for v in totals])
+                )
+                lines = [jnp.sum(v, axis=0, keepdims=True) for v in sums]
+                lines += [ba, be, jnp.sum(excess, axis=0, keepdims=True)]
+                lines += [jnp.zeros((2, cells), F32)]
+                value = jnp.sum(jnp.concatenate(lines, axis=0), axis=1, keepdims=True)
+                value = jnp.where(seat == spot, jnp.broadcast_to(value, (8, cells)), 0.0)
+                sends += begin(0, jnp.sum(value, axis=0, keepdims=True))
             block = jnp.concatenate([coupled[c, d] for d in range(nz)], axis=1)
             spread = jnp.dot(
                 block, pick[c, :, s * quad:span * cells], preferred_element_type=F32
@@ -658,60 +807,20 @@
                 back[pl.ds(x, full, stride=rows), :] = spread[:, i * cells:(i + 1) * cells]
             if s + 1 < per:
                 partial[:, (s + 1) * quad:span * cells] = spread[:, quad:]
-        part = weight[h * span:(h + 1) * span, :]
-
-        def image(j, carry):
-            ba, be = carry
-            b = b_ref[j, h * span:(h + 1) * span, :].astype(F32)
-            images = []
-            for f in range(2):
-                q = f * slab + j
-                coup = back[pl.ds(pl.multiple_of(q * rows + h * span, 8), span), :]
-                images.append(part * (coup + before_image[q, h * span:(h + 1) * span, :]))
-                outs[f][j, h * span:(h + 1) * span, :] = images[f].astype(BF16)
-            return ba + b * images[0], be + b * images[1]
-
-        pair = lax.fori_loop(0, slab, image, pair, unroll=6)
-
-    lines = [jnp.sum(v, axis=0, keepdims=True) for v in (*sums, *pair, excess)]
-    value = jnp.concatenate(lines + [jnp.zeros((2, cells), F32)], axis=0)
-    base = 0
-    plane = [(i, k) for i in range(ny) for k in range(nx)]
-    stages = (
-        ([{"lz": lax.rem(mz + k, nz)} for k in range(nz)], nz, stat_z, sr_z, mz,
-         [lax.rem(mz + nz - k, nz) for k in range(nz)]),
-        ([{"ty": lax.rem(my + i, ny), "tx": lax.rem(mx + k, nx)} for i, k in plane],
-         ny * nx, stat_y, sr_y, my * nx + mx,
-         [lax.rem(my + ny - i, ny) * nx + lax.rem(mx + nx - k, nx) for i, k in plane]),
-    )
-    sends = []
-    for s, (peers, size, box, sem, me, sources) in enumerate(stages):
-        stat_out[s] = value
-        box[me] = value
-        for k in range(1, size):
-            copy = pltpu.make_async_remote_copy(
-                src_ref=stat_out.at[s], dst_ref=box.at[me], send_sem=ss.at[base + k - 1],
-                recv_sem=sem.at[me], device_id=peers[k], device_id_type=MESH,
-            )
-            copy.start()
-            sends.append(copy)
-        base += size - 1
-        for k in range(1, size):
-            src = sources[k]
-            pltpu.make_async_remote_copy(
-                src_ref=stat_out.at[s], dst_ref=box.at[src], send_sem=ss.at[0],
-                recv_sem=sem.at[src], device_id=peers[k], device_id_type=MESH,
-            ).wait_recv()
-        value = box[0]
-        for i in range(1, size):
-            value = value + box[i]
-    final = jnp.broadcast_to(jnp.sum(value, axis=1, keepdims=True), (8, cells))
-    bb, cc, cv, ba, be, over = (final[i:i + 1] for i in range(6))
-    line = lax.broadcasted_iota(jnp.int32, (1, cells), 1)
-    top = jnp.where(line == 0, ba, jnp.where(line == 1, be, cv))
-    low = jnp.where(line == 2, cc, bb)
-    border_ref[...] = top / jnp.sqrt(low)
-    flag_ref[0] = jnp.where(jnp.max(over) > 0.0, 1, 0)
+            ready = (nz * s + done) // 8 * 8
+            if s == per - 1 or (h == halves - 1 and s == per - 2 and ready > drawn):
+                image(h * span + drawn, h * span + ready)
+                drawn = ready
+
+    value = finish(0)
+    for s in range(1, stages):
+        sends += begin(s, value)
+        value = finish(s)
+    value = jnp.broadcast_to(value, (8, cells))
+    top = jnp.where(spot < 2, pltpu.roll(value, cells - 3, 1), value)
+    low = jnp.where(spot == 0, value, pltpu.roll(value, 1, 1))
+    border_ref[...] = (top / jnp.sqrt(low))[:1]
+    flag_ref[0] = jnp.where(jnp.sum(jnp.where(spot == 5, value, 0.0)) > 0.0, 1, 0)
 
     for c in range(chunks):
         for k in order:
@@ -784,6 +893,7 @@
     full = 2 * slab
     chunks = (rows * 3 // 4) // nz
     quad = nz * cells
+    groups = [math.prod(n for _, _, n in dims) for dims in stage_sizes(sizes)]
     vmem = pl.BlockSpec(memory_space=pltpu.VMEM)
     smem = pl.BlockSpec(memory_space=pltpu.SMEM)
     hbm = pl.BlockSpec(memory_space=pl.ANY)
@@ -796,20 +906,23 @@
             jax.ShapeDtypeStruct((1, cells), F32),
             jax.ShapeDtypeStruct((1,), jnp.int32),
         ),
-        in_specs=[hbm] * 4 + [vmem] * 2 + [hbm] * 2 + [smem],
+        in_specs=[hbm] * 4 + [vmem] * 2 + [hbm] * 3,
         out_specs=(vmem, vmem, vmem, smem),
         scratch_shapes=[
             *[pltpu.VMEM((slab, rows, cells), BF16)] * 4,
             pltpu.VMEM(args[6].shape, BF16),
             pltpu.VMEM(args[7].shape, BF16),
-            pltpu.VMEM((rows // span, full, span * cells), BF16),
+            pltpu.SMEM(args[8].shape, F32),
+            pltpu.VMEM((rows // span, full + slab, span * cells), BF16),
             pltpu.VMEM((chunks, quad, span * cells), BF16),
-            *[pltpu.VMEM((chunks, nz, full, cells), BF16)] * 4,
+            *[pltpu.VMEM((chunks, nz, full + slab, cells), BF16)] * 2,
+            *[pltpu.VMEM((chunks, nz, full, cells), BF16)] * 2,
             pltpu.VMEM((full, span * cells), F32),
             pltpu.VMEM((rows, cells), F32),
             pltpu.VMEM((rows, cells), F32),
             pltpu.VMEM((nz * full, nz * full), BF16),
             pltpu.VMEM((full * (rows + 2 * MARGIN), cells), F32),
+            pltpu.VMEM((slab * rows, cells), F32),
             pltpu.VMEM((full * rows, cells), F32),
             pltpu.VMEM((full, rows, cells), F32),
             pltpu.VMEM((2, full, cells), BF16),
@@ -817,15 +930,13 @@
             pltpu.VMEM((2, 2, rows, cells), BF16),
             pltpu.VMEM((2, 2, rows, cells), BF16),
             pltpu.VMEM((2, 2, rows, cells), F32),
-            pltpu.VMEM((2, 8, cells), F32),
-            pltpu.VMEM((nz, 8, cells), F32),
-            pltpu.VMEM((ny * nx, 8, cells), F32),
-            dma((6,)),
+            pltpu.VMEM((len(groups), 1, cells), F32),
+            *[pltpu.VMEM((n, 1, cells), F32) for n in groups],
+            dma((7,)),
             *[dma((chunks, nz))] * 4,
             *[dma((2,))] * 4,
-            dma((nx * ny + nz - 2,)),
-            dma((nz,)),
-            dma((ny * nx,)),
+            dma((sum(groups) - len(groups),)),
+            *[dma((n,)) for n in groups],
         ],
         compiler_params=pltpu.CompilerParams(
             collective_id=1, has_side_effects=True, vmem_limit_bytes=52 * 1024 * 1024
@@ -839,19 +950,20 @@
     slab = units * layers
     wide = [v.transpose(1, 2, 0, 3).reshape(slab, rows, cells) for v in arrays[:4]]
     args = (*wide, arrays[4], arrays[5].T, arrays[6].transpose(1, 0, 2), *arrays[7:])
-    args = (*[pltpu.with_memory_space_constraint(v, pltpu.HBM) for v in args[:8]], args[8])
+    held = [pltpu.with_memory_space_constraint(v, pltpu.HBM) for v in args]
     span = rows // 2
     if rows % 16 == 0 and (span * 3 // 4) % nz == 0:
-        *quick, flag = fast_call(sizes, span, units, layers, args)
+        *quick, flag = fast_call(sizes, span, units, layers, held)
         out_t, out_d, border = lax.cond(
-            flag[0] > 0, lambda: dense_call(sizes, units, layers, args), lambda: tuple(quick)
+            flag[0] > 0, lambda: dense_call(sizes, units, layers, held), lambda: tuple(quick)
         )
     else:
-        out_t, out_d, border = dense_call(sizes, units, layers, args)
+        out_t, out_d, border = dense_call(sizes, units, layers, held)
+    out_t, out_d, border = put_call(out_t, out_d, border)
     outs = [
         v.reshape(units, layers, rows, cells).transpose(2, 0, 1, 3) for v in (out_t, out_d)
     ]
-    return (*outs, border[0, :3])
+    return (*outs, border)
 
 
 def solution(mesh):

time: 61.9 us -> 56.8 us (0.918)
  local copies, waits for them, and re-layouts: 2.79 us -> 0 us
  Pallas kernels: 57.3 us -> 55.1 us
    pallas_call x1, Pallas kernels: 57.3 us -> 54.1 us  [fast_call(): pl.pallas_call(functools.partial(fast_kernel, sizes, span, units), out_sh...]
    unnamed x4 -> x0, local copies, waits for them, and re-layouts: 2.28 us -> none
    pallas_call x0 -> x1, Pallas kernels: none -> 1.04 us  [put_call(): pl.pallas_call(put_kernel, out_shape=(jax.ShapeDtypeStruct(out_t.shape, B...]
where the time goes in v1:
time: 56.8 us; the launch traced here: 56.6 us
  Pallas kernels  55.1 us (97%)
  between operations  1.42 us (2%)
    pallas_call x1, Pallas kernels, fast_call(): pl.pallas_call(functools.partial(fast_kernel, sizes, span, units), out_sh...  54.1 us

profile of v1, /device:TPU:0, one launch (start us, length us, event | category | flops | bytes accessed | tf_op | source)
XLA Modules:
  0.0 56.6 jit_solution(10870742976971901767)
XLA Ops:
  0.6 54.1 %shard_map.112 = (bf16[72,32,128]{2,1,0:T(8,128)(2,1)S(1)}, bf16[72,32,128]{2,1,0:T(8,128)(2,1)S(1)}, f32[1,128]{1,0:T(1,128)S(1)}, s32[1]{0:T(128)}) custom-call(bf16[72,32,128]{2,1,0:T(8,128)(2,1)} %bitcast.21, bf16[72,32,128]{2,1,0:T(8,128)(2,1)} %bitcast.23, bf16[72,32,128]{2,1,0:T(8,128)(2,1)} %bitcast.25, bf16[72,32,128]{2,1,0:T(8,128)(2,1)} %bitcast.27, ...), custom_call_target="tpu_custom_call" | custom-call | tf_op jit(solution)/shard_map/pallas_call | solution.py:901
  55.4 1.0 %shard_map.113 = (bf16[72,32,128]{2,1,0:T(8,128)(2,1)}, bf16[72,32,128]{2,1,0:T(8,128)(2,1)}, f32[3]{0:T(128)}) custom-call(bf16[72,32,128]{2,1,0:T(8,128)(2,1)S(1)} %get-tuple-element.50.t_ref, bf16[72,32,128]{2,1,0:T(8,128)(2,1)S(1)} %get-tuple-element.51.d_ref, f32[1,128]{1,0:T(1,128)S(1)} %get-tuple-element.52.border_ref), custom_call_target="tpu_custom_call" | custom-call | tf_op jit(solution)/shard_map/pallas_call | solution.py:382
  (1 shorter events, 0.0 us)

commit v2 on v1

--- a/solution.py
+++ b/solution.py
@@ -405,7 +405,7 @@
     stages = len(stage_sizes(sizes))
     boxes, rest = rest[:stages], rest[stages:]
     ls, fs, fr, bs, br, xs, xr, ys, yr, ss = rest[:10]
-    stat_sems = rest[10:]
+    stat_sems = rest[10]
     slab, rows, cells = test_ref.shape
     layers = slab // units
     full = 2 * slab
@@ -511,29 +511,30 @@
         for d in range(nz):
             packed[c, d] = found[:, d * cells:(d + 1) * cells]
 
-    def sent(c):
-        return full if c < chunks - 1 else full + slab
+    def target(k):
+        down = nz - k
+        low = down - jnp.where(down <= mz, 1, 0)
+        high = k - 1 + jnp.where(k - 1 >= mz, 1, 0)
+        return jnp.where(mz < nz // 2, low, high)
 
     def forward(c, k):
-        to = lax.rem(mz + k, nz)
-        part = pl.ds(0, sent(c))
+        to = target(k)
         return pltpu.make_async_remote_copy(
-            src_ref=packed.at[c, to, part], dst_ref=arrived.at[c, mz, part],
+            src_ref=packed.at[c, to, pl.ds(0, full)], dst_ref=arrived.at[c, mz],
             send_sem=fs.at[c, to], recv_sem=fr.at[c, mz], device_id={"lz": to},
             device_id_type=MESH,
         )
 
     def forward_in(c, k):
         src = lax.rem(mz + nz - k, nz)
-        part = pl.ds(0, sent(c))
         return pltpu.make_async_remote_copy(
-            src_ref=arrived.at[c, src, part], dst_ref=arrived.at[c, src, part],
+            src_ref=arrived.at[c, src], dst_ref=arrived.at[c, src],
             send_sem=fs.at[c, src], recv_sem=fr.at[c, src], device_id={"lz": src},
             device_id_type=MESH,
         )
 
     def backward(c, k):
-        to = lax.rem(mz + k, nz)
+        to = target(k)
         return pltpu.make_async_remote_copy(
             src_ref=product.at[c, to], dst_ref=coupled.at[c, mz], send_sem=bs.at[c, to],
             recv_sem=br.at[c, mz], device_id={"lz": to}, device_id_type=MESH,
@@ -546,7 +547,7 @@
             recv_sem=br.at[c, src], device_id={"lz": src}, device_id_type=MESH,
         )
 
-    order = sorted(range(1, nz), key=lambda k: -min(k, nz - k))
+    order = range(1, nz)
     for load in loads[:3]:
         load.wait()
     for h in range(halves):
@@ -560,7 +561,7 @@
                 pl.semaphore_wait(barrier, nx * ny + nz - 2)
             for k in order:
                 forward(c, k).start()
-            arrived[c, mz] = packed[c, mz]
+            arrived[c, mz] = packed[c, mz, :full]
 
     halo_out[0] = wide_ref[halves - 1, :full, (span - 1) * cells:span * cells]
     halo_out[1] = wide_ref[0, :full, :cells]
@@ -703,15 +704,13 @@
     for c in range(chunks):
         for k in order:
             forward_in(c, k).wait_recv()
-        part = jnp.concatenate([arrived[c, d, :full] for d in range(nz)], axis=0)
+        part = arrived[c].reshape(wide, cells)
         result = jnp.dot(big_k[...], part, preferred_element_type=F32).astype(BF16)
         for d in range(nz):
             product[c, d] = result[d * full:(d + 1) * full]
         for k in order:
             backward(c, k).start()
         coupled[c, mz] = product[c, mz]
-        if sent(c) > full:
-            pair = dots(pair, product.at[c], arrived.at[c])
         sums = lax.fori_loop(c * share, (c + 1) * share, norms, sums, unroll=2)
         for job in jobs[c * each:(c + 1) * each]:
             local_part(*job)
@@ -735,23 +734,18 @@
         stat_out[s] = value
         _, peers, me = reduce_stages[s]
         boxes[s][me] = value
-        copies = []
-        for n, (peer, source) in enumerate(peers):
-            copy = pltpu.make_async_remote_copy(
-                src_ref=stat_out.at[s], dst_ref=boxes[s].at[me], send_sem=ss.at[bases[s] + n],
-                recv_sem=stat_sems[s].at[me], device_id=peer, device_id_type=MESH,
-            )
-            copy.start()
-            copies.append(copy)
-        return copies
+        for peer in peers:
+            pltpu.make_async_remote_copy(
+                src_ref=stat_out.at[s], dst_ref=boxes[s].at[me], send_sem=ss.at[s],
+                recv_sem=stat_sems.at[s], device_id=peer, device_id_type=MESH,
+            ).start()
+
+    def every(s, sem):
+        rows_in = boxes[s].at[pl.ds(0, len(reduce_stages[s][1]))]
+        return pltpu.make_async_copy(rows_in, rows_in, sem.at[s])
 
     def finish(s):
-        for n, (peer, source) in enumerate(reduce_stages[s][1]):
-            pltpu.make_async_remote_copy(
-                src_ref=stat_out.at[s], dst_ref=boxes[s].at[source],
-                send_sem=ss.at[bases[s] + n], recv_sem=stat_sems[s].at[source], device_id=peer,
-                device_id_type=MESH,
-            ).wait_recv()
+        every(s, stat_sems).wait()
         return jnp.sum(boxes[s][...], axis=0)
 
     reduce_stages = []
@@ -766,13 +760,8 @@
                     name: lax.rem(lax.axis_index(name) + k, n)
                     for (name, _, n), k in zip(dims, shift)
                 }
-                source = 0
-                for (name, _, n), k in zip(dims, shift):
-                    source = source * n + lax.rem(lax.axis_index(name) + n - k, n)
-                peers.append((peer, source))
+                peers.append(peer)
         reduce_stages.append((dims, peers, me))
-    bases = [sum(len(r[1]) for r in reduce_stages[:s]) for s in range(stages)]
-    sends = []
 
     seat = lax.broadcasted_iota(jnp.int32, (8, cells), 0)
     spot = lax.broadcasted_iota(jnp.int32, (8, cells), 1)
@@ -782,9 +771,8 @@
             c = h * per + s
             for k in order:
                 backward_in(c, k).wait_recv()
-            if sent(c) == full:
-                pair = dots(pair, coupled.at[c], packed.at[c])
-            if c == chunks - 2:
+            pair = dots(pair, coupled.at[c], packed.at[c])
+            if c == chunks - 1:
                 ba, be = (
                     jnp.sum(v, axis=0, keepdims=True) + jnp.sum(w, axis=0, keepdims=True)
                     for v, w in zip(pair, [ocean * v for v in totals])
@@ -794,7 +782,7 @@
                 lines += [jnp.zeros((2, cells), F32)]
                 value = jnp.sum(jnp.concatenate(lines, axis=0), axis=1, keepdims=True)
                 value = jnp.where(seat == spot, jnp.broadcast_to(value, (8, cells)), 0.0)
-                sends += begin(0, jnp.sum(value, axis=0, keepdims=True))
+                begin(0, jnp.sum(value, axis=0, keepdims=True))
             block = jnp.concatenate([coupled[c, d] for d in range(nz)], axis=1)
             spread = jnp.dot(
                 block, pick[c, :, s * quad:span * cells], preferred_element_type=F32
@@ -814,7 +802,7 @@
 
     value = finish(0)
     for s in range(1, stages):
-        sends += begin(s, value)
+        begin(s, value)
         value = finish(s)
     value = jnp.broadcast_to(value, (8, cells))
     top = jnp.where(spot < 2, pltpu.roll(value, cells - 3, 1), value)
@@ -830,8 +818,8 @@
     to_before.wait_send()
     to_up.wait_send()
     to_down.wait_send()
-    for copy in sends:
-        copy.wait_send()
+    for s in range(stages):
+        every(s, ss).wait()
 
 
 def dense_call(sizes, units, layers, args):
@@ -915,8 +903,8 @@
             pltpu.SMEM(args[8].shape, F32),
             pltpu.VMEM((rows // span, full + slab, span * cells), BF16),
             pltpu.VMEM((chunks, quad, span * cells), BF16),
-            *[pltpu.VMEM((chunks, nz, full + slab, cells), BF16)] * 2,
-            *[pltpu.VMEM((chunks, nz, full, cells), BF16)] * 2,
+            pltpu.VMEM((chunks, nz, full + slab, cells), BF16),
+            *[pltpu.VMEM((chunks, nz, full, cells), BF16)] * 3,
             pltpu.VMEM((full, span * cells), F32),
             pltpu.VMEM((rows, cells), F32),
             pltpu.VMEM((rows, cells), F32),
@@ -935,8 +923,7 @@
             dma((7,)),
             *[dma((chunks, nz))] * 4,
             *[dma((2,))] * 4,
-            dma((sum(groups) - len(groups),)),
-            *[dma((n,)) for n in groups],
+            *[dma((len(groups),))] * 2,
         ],
         compiler_params=pltpu.CompilerParams(
             collective_id=1, has_side_effects=True, vmem_limit_bytes=52 * 1024 * 1024

time: 56.8 us -> 55.9 us (0.984)
  Pallas kernels: 55.1 us -> 54 us
    pallas_call x1, Pallas kernels: 54.1 us -> 52.9 us  [fast_call(): pl.pallas_call(functools.partial(fast_kernel, sizes, span, units), out_sh...]
where the time goes in v2:
time: 55.9 us; the launch traced here: 55.6 us
  Pallas kernels  54 us (97%)
  between operations  1.44 us (3%)
    pallas_call x1, Pallas kernels, fast_call(): pl.pallas_call(functools.partial(fast_kernel, sizes, span, units), out_sh...  52.9 us

profile of v2, /device:TPU:0, one launch (start us, length us, event | category | flops | bytes accessed | tf_op | source)
XLA Modules:
  0.0 55.6 jit_solution(194463276020165810)
XLA Ops:
  0.6 52.9 %shard_map.112 = (bf16[72,32,128]{2,1,0:T(8,128)(2,1)S(1)}, bf16[72,32,128]{2,1,0:T(8,128)(2,1)S(1)}, f32[1,128]{1,0:T(1,128)S(1)}, s32[1]{0:T(128)}) custom-call(bf16[72,32,128]{2,1,0:T(8,128)(2,1)} %bitcast.21, bf16[72,32,128]{2,1,0:T(8,128)(2,1)} %bitcast.23, bf16[72,32,128]{2,1,0:T(8,128)(2,1)} %bitcast.25, bf16[72,32,128]{2,1,0:T(8,128)(2,1)} %bitcast.27, ...), custom_call_target="tpu_custom_call" | custom-call | tf_op jit(solution)/shard_map/pallas_call | solution.py:889
  54.2 0.2 conditional.1
  54.4 1.0 %shard_map.113 = (bf16[72,32,128]{2,1,0:T(8,128)(2,1)}, bf16[72,32,128]{2,1,0:T(8,128)(2,1)}, f32[3]{0:T(128)}) custom-call(bf16[72,32,128]{2,1,0:T(8,128)(2,1)S(1)} %get-tuple-element.50.t_ref, bf16[72,32,128]{2,1,0:T(8,128)(2,1)S(1)} %get-tuple-element.51.d_ref, f32[1,128]{1,0:T(1,128)S(1)} %get-tuple-element.52.border_ref), custom_call_target="tpu_custom_call" | custom-call | tf_op jit(solution)/shard_map/pallas_call | solution.py:382

commit v3 on v2

--- a/solution.py
+++ b/solution.py
@@ -397,7 +397,7 @@
     test_hbm, dir_hbm, b_hbm, c_hbm, land_ref, active_ref, blocks_hbm, k_hbm, kappa_hbm,
     out_t, out_d, border_ref, flag_ref,
     test_ref, dir_ref, b_ref, c_ref, blocks_ref, k_ref,
-    kappa_ref, wide_ref, pick, packed, arrived, product, coupled, partial, weight, place, big_k,
+    kappa_ref, wide_ref, wide_b, pick, packed, packed_b, arrived, product, coupled, partial, weight, place, big_k,
     field, b_field, back, before_image, halo_out, halo, edge_out, edge_in, edge_f, stat_out,
     *rest,
 ):
@@ -485,31 +485,37 @@
 
             lax.fori_loop(0, slab, mask, 0, unroll=8)
 
-        def widen(j, carry):
-            start = pl.multiple_of(j * rows + h * span, 8)
-            b_field[pl.ds(start, span), :] = b_ref[j, h * span:(h + 1) * span, :].astype(F32)
-            return carry
-
-        lax.fori_loop(0, slab, widen, 0, unroll=8)
-
         def pack_row(i, carry):
             spot = pl.ds(pl.multiple_of(i * cells, cells), cells)
             row = field[pl.ds(MARGIN + h * span + i, full, stride=pitch), :].astype(BF16)
-            wide_ref[h, :full, spot] = row
-            row = b_field[pl.ds(h * span + i, slab, stride=rows), :].astype(BF16)
-            wide_ref[h, full:, spot] = row
+            wide_ref[h, :, spot] = row
             return carry
 
         lax.fori_loop(0, span, pack_row, 0, unroll=4)
 
-    def compact(h, s):
+    def prepare_b():
+        def widen(j, carry):
+            start = pl.multiple_of(j * rows, 8)
+            b_field[pl.ds(start, rows), :] = b_ref[j].astype(F32)
+            return carry
+
+        lax.fori_loop(0, slab, widen, 0, unroll=4)
+        for h in range(halves):
+            def pack_row(i, carry):
+                row = b_field[pl.ds(h * span + i, slab, stride=rows), :].astype(BF16)
+                wide_b[h, :, pl.ds(pl.multiple_of(i * cells, cells), cells)] = row
+                return carry
+
+            lax.fori_loop(0, span, pack_row, 0, unroll=4)
+
+    def compact(h, s, source, target):
         c = h * per + s
         found = lax.dot_general(
-            wide_ref[h, :, s * quad:span * cells], pick[c, :, s * quad:span * cells],
+            source[h, :, s * quad:span * cells], pick[c, :, s * quad:span * cells],
             (((1,), (1,)), ((), ())), preferred_element_type=F32,
         ).astype(BF16)
         for d in range(nz):
-            packed[c, d] = found[:, d * cells:(d + 1) * cells]
+            target[c, d] = found[:, d * cells:(d + 1) * cells]
 
     def target(k):
         down = nz - k
@@ -520,7 +526,7 @@
     def forward(c, k):
         to = target(k)
         return pltpu.make_async_remote_copy(
-            src_ref=packed.at[c, to, pl.ds(0, full)], dst_ref=arrived.at[c, mz],
+            src_ref=packed.at[c, to], dst_ref=arrived.at[c, mz],
             send_sem=fs.at[c, to], recv_sem=fr.at[c, mz], device_id={"lz": to},
             device_id_type=MESH,
         )
@@ -548,23 +554,23 @@
         )
 
     order = range(1, nz)
-    for load in loads[:3]:
-        load.wait()
+    loads[0].wait()
+    loads[1].wait()
     for h in range(halves):
         prepare(h)
         for s in range(per):
             c = h * per + s
             if c:
                 choose(h, s)
-            compact(h, s)
+            compact(h, s, wide_ref, packed)
             if c == 0:
                 pl.semaphore_wait(barrier, nx * ny + nz - 2)
             for k in order:
                 forward(c, k).start()
-            arrived[c, mz] = packed[c, mz, :full]
-
-    halo_out[0] = wide_ref[halves - 1, :full, (span - 1) * cells:span * cells]
-    halo_out[1] = wide_ref[0, :full, :cells]
+            arrived[c, mz] = packed[c, mz]
+
+    halo_out[0] = wide_ref[halves - 1, :, (span - 1) * cells:span * cells]
+    halo_out[1] = wide_ref[0, :, :cells]
     later, before = lax.rem(mx + 1, nx), lax.rem(mx + nx - 1, nx)
     to_later = pltpu.make_async_remote_copy(
         src_ref=halo_out.at[0], dst_ref=halo.at[0], send_sem=xs.at[0], recv_sem=xr.at[0],
@@ -623,6 +629,7 @@
         total = both if total is None else total + both
     big_k[...] = total.astype(BF16)
 
+    loads[2].wait()
     for load in loads[4:]:
         load.wait()
     zero = jnp.zeros((rows, cells), F32)
@@ -694,7 +701,7 @@
         ba, be = pair
         for d in range(nz):
             y = values[d].astype(F32)
-            b = weights[d, full:].astype(F32)
+            b = weights[d].astype(F32)
             ba = ba + jnp.sum((y[:slab] * b).reshape(slab // 8, 8, cells), axis=0)
             be = be + jnp.sum((y[slab:] * b).reshape(slab // 8, 8, cells), axis=0)
         return ba, be
@@ -712,6 +719,9 @@
             backward(c, k).start()
         coupled[c, mz] = product[c, mz]
         sums = lax.fori_loop(c * share, (c + 1) * share, norms, sums, unroll=2)
+        if c == 0:
+            prepare_b()
+        compact(c // per, c % per, wide_b, packed_b)
         for job in jobs[c * each:(c + 1) * each]:
             local_part(*job)
     if share * chunks < slab:
@@ -734,7 +744,7 @@
         stat_out[s] = value
         _, peers, me = reduce_stages[s]
         boxes[s][me] = value
-        for peer in peers:
+        for peer in reversed(peers):
             pltpu.make_async_remote_copy(
                 src_ref=stat_out.at[s], dst_ref=boxes[s].at[me], send_sem=ss.at[s],
                 recv_sem=stat_sems.at[s], device_id=peer, device_id_type=MESH,
@@ -765,24 +775,27 @@
 
     seat = lax.broadcasted_iota(jnp.int32, (8, cells), 0)
     spot = lax.broadcasted_iota(jnp.int32, (8, cells), 1)
+
+    def line_of(values):
+        lines = [jnp.sum(v, axis=0, keepdims=True) for v in values]
+        lines += [jnp.zeros((8 - len(lines), cells), F32)]
+        value = jnp.sum(jnp.concatenate(lines, axis=0), axis=1, keepdims=True)
+        value = jnp.where(seat == spot, jnp.broadcast_to(value, (8, cells)), 0.0)
+        return jnp.sum(value, axis=0, keepdims=True)
+
     for h in range(halves):
         drawn = 0
         for s in range(per):
             c = h * per + s
+            if c == chunks - 1:
+                early = line_of((*sums, *(ocean * v for v in totals), excess))
+                early = early + line_of((tile, tile, tile, *pair, tile))
+                pair = (tile, tile)
             for k in order:
                 backward_in(c, k).wait_recv()
-            pair = dots(pair, coupled.at[c], packed.at[c])
+            pair = dots(pair, coupled.at[c], packed_b.at[c])
             if c == chunks - 1:
-                ba, be = (
-                    jnp.sum(v, axis=0, keepdims=True) + jnp.sum(w, axis=0, keepdims=True)
-                    for v, w in zip(pair, [ocean * v for v in totals])
-                )
-                lines = [jnp.sum(v, axis=0, keepdims=True) for v in sums]
-                lines += [ba, be, jnp.sum(excess, axis=0, keepdims=True)]
-                lines += [jnp.zeros((2, cells), F32)]
-                value = jnp.sum(jnp.concatenate(lines, axis=0), axis=1, keepdims=True)
-                value = jnp.where(seat == spot, jnp.broadcast_to(value, (8, cells)), 0.0)
-                begin(0, jnp.sum(value, axis=0, keepdims=True))
+                begin(0, early + line_of((tile, tile, tile, *pair, tile)))
             block = jnp.concatenate([coupled[c, d] for d in range(nz)], axis=1)
             spread = jnp.dot(
                 block, pick[c, :, s * quad:span * cells], preferred_element_type=F32
@@ -901,9 +914,11 @@
             pltpu.VMEM(args[6].shape, BF16),
             pltpu.VMEM(args[7].shape, BF16),
             pltpu.SMEM(args[8].shape, F32),
-            pltpu.VMEM((rows // span, full + slab, span * cells), BF16),
+            pltpu.VMEM((rows // span, full, span * cells), BF16),
+            pltpu.VMEM((rows // span, slab, span * cells), BF16),
             pltpu.VMEM((chunks, quad, span * cells), BF16),
-            pltpu.VMEM((chunks, nz, full + slab, cells), BF16),
+            pltpu.VMEM((chunks, nz, full, cells), BF16),
+            pltpu.VMEM((chunks, nz, slab, cells), BF16),
             *[pltpu.VMEM((chunks, nz, full, cells), BF16)] * 3,
             pltpu.VMEM((full, span * cells), F32),
             pltpu.VMEM((rows, cells), F32),

time: 55.9 us -> 55.3 us (0.989)
  no operation moved by 1% of the time
where the time goes in v3:
time: 55.3 us; the launch traced here: 55 us
  Pallas kernels  53.6 us (97%)
  between operations  1.42 us (3%)
    pallas_call x1, Pallas kernels, fast_call(): pl.pallas_call(functools.partial(fast_kernel, sizes, span, units), out_sh...  52.6 us

profile of v3, /device:TPU:0, one launch (start us, length us, event | category | flops | bytes accessed | tf_op | source)
XLA Modules:
  0.0 55.0 jit_solution(13883842294741478869)
XLA Ops:
  0.6 52.6 %shard_map.112 = (bf16[72,32,128]{2,1,0:T(8,128)(2,1)S(1)}, bf16[72,32,128]{2,1,0:T(8,128)(2,1)S(1)}, f32[1,128]{1,0:T(1,128)S(1)}, s32[1]{0:T(128)}) custom-call(bf16[72,32,128]{2,1,0:T(8,128)(2,1)} %bitcast.21, bf16[72,32,128]{2,1,0:T(8,128)(2,1)} %bitcast.23, bf16[72,32,128]{2,1,0:T(8,128)(2,1)} %bitcast.25, bf16[72,32,128]{2,1,0:T(8,128)(2,1)} %bitcast.27, ...), custom_call_target="tpu_custom_call" | custom-call | tf_op jit(solution)/shard_map/pallas_call | solution.py:902
  53.8 1.0 %shard_map.113 = (bf16[72,32,128]{2,1,0:T(8,128)(2,1)}, bf16[72,32,128]{2,1,0:T(8,128)(2,1)}, f32[3]{0:T(128)}) custom-call(bf16[72,32,128]{2,1,0:T(8,128)(2,1)S(1)} %get-tuple-element.50.t_ref, bf16[72,32,128]{2,1,0:T(8,128)(2,1)S(1)} %get-tuple-element.51.d_ref, f32[1,128]{1,0:T(1,128)S(1)} %get-tuple-element.52.border_ref), custom_call_target="tpu_custom_call" | custom-call | tf_op jit(solution)/shard_map/pallas_call | solution.py:382
  (1 shorter events, 0.0 us)

commit v4 on v3

--- a/solution.py
+++ b/solution.py
@@ -813,6 +813,14 @@
                 image(h * span + drawn, h * span + ready)
                 drawn = ready
 
+    for c in range(chunks):
+        for k in order:
+            forward(c, k).wait_send()
+            backward(c, k).wait_send()
+    to_later.wait_send()
+    to_before.wait_send()
+    to_up.wait_send()
+    to_down.wait_send()
     value = finish(0)
     for s in range(1, stages):
         begin(s, value)
@@ -823,14 +831,6 @@
     border_ref[...] = (top / jnp.sqrt(low))[:1]
     flag_ref[0] = jnp.where(jnp.sum(jnp.where(spot == 5, value, 0.0)) > 0.0, 1, 0)
 
-    for c in range(chunks):
-        for k in order:
-            forward(c, k).wait_send()
-            backward(c, k).wait_send()
-    to_later.wait_send()
-    to_before.wait_send()
-    to_up.wait_send()
-    to_down.wait_send()
     for s in range(stages):
         every(s, ss).wait()
 

time: 55.3 us -> 55.2 us (level)
  no operation moved by 1% of the time
where the time goes in v4:
time: 55.2 us; the launch traced here: 55 us
  Pallas kernels  53.5 us (97%)
  between operations  1.42 us (3%)
    pallas_call x1, Pallas kernels, fast_call(): pl.pallas_call(functools.partial(fast_kernel, sizes, span, units), out_sh...  52.5 us

profile of v4, /device:TPU:0, one launch (start us, length us, event | category | flops | bytes accessed | tf_op | source)
XLA Modules:
  0.0 55.0 jit_solution(10229350163974875202)
XLA Ops:
  0.6 52.5 %shard_map.112 = (bf16[72,32,128]{2,1,0:T(8,128)(2,1)S(1)}, bf16[72,32,128]{2,1,0:T(8,128)(2,1)S(1)}, f32[1,128]{1,0:T(1,128)S(1)}, s32[1]{0:T(128)}) custom-call(bf16[72,32,128]{2,1,0:T(8,128)(2,1)} %bitcast.21, bf16[72,32,128]{2,1,0:T(8,128)(2,1)} %bitcast.23, bf16[72,32,128]{2,1,0:T(8,128)(2,1)} %bitcast.25, bf16[72,32,128]{2,1,0:T(8,128)(2,1)} %bitcast.27, ...), custom_call_target="tpu_custom_call" | custom-call | tf_op jit(solution)/shard_map/pallas_call | solution.py:902
  53.8 1.0 %shard_map.113 = (bf16[72,32,128]{2,1,0:T(8,128)(2,1)}, bf16[72,32,128]{2,1,0:T(8,128)(2,1)}, f32[3]{0:T(128)}) custom-call(bf16[72,32,128]{2,1,0:T(8,128)(2,1)S(1)} %get-tuple-element.50.t_ref, bf16[72,32,128]{2,1,0:T(8,128)(2,1)S(1)} %get-tuple-element.51.d_ref, f32[1,128]{1,0:T(1,128)S(1)} %get-tuple-element.52.border_ref), custom_call_target="tpu_custom_call" | custom-call | tf_op jit(solution)/shard_map/pallas_call | solution.py:382
  (1 shorter events, 0.0 us)
